TPU v7x, 256 devices: a whole 4x4x8 slice. The times are simulated.
256 devices in a mesh: strip: 64 (over x, z, core), chan: 4 (over y).
Axes of the slice: x: 4, y: 4, z: 8, core: 2. Of those that a mesh axis runs over, the one named last changes fastest.
Arguments:
- section_input: bfloat16 [48, 8192, 256], P(None, 'strip'), may hold values from -6 to 6
- conv_weight: bfloat16 [3, 3, 256, 256], replicated, may hold values from -0.125 to 0.125
- conv_bias: float32 [256], replicated, may hold values from -3 to 3
- deep_weight: bfloat16 [3, 3, 256, 512], P(None, None, None, 'chan'), may hold values from -0.125 to 0.125
- deep_bias: float32 [512], P('chan'), may hold values from -3 to 3
- labels: int32 [24, 4096], P(None, 'strip'), may hold values from 0 to 32, as said below
- slot_ids: int32 [2048], P('strip'), may hold values from 0 to 4095, as said below
- embed_grad: float32 [4096, 512], P('strip', 'chan'), may hold values from -0.8 to 0.8
Outputs:
- embeddings: float32 [4096, 512], P('strip', 'chan')
- weight_grad: float32 [3, 3, 256, 512], P(None, None, None, 'chan')
- bias_grad: float32 [512], P('chan')
Inputs may be any that keep to these rules, and one draw needn't show every extreme that they name: `labels`: the value 32 marks background; any other value v names entry v of the list of the strip that holds the pixel. `slot_ids`: A value s names slot s % 64 of owner s // 64 (an index of strip). The slots within one strip's list differ; a slot stands in the lists of at most two strips, which are neighbours (a crack across a strip border). Every owner holds at most 64 components and some owner holds exactly 64.
All inputs are finite; a program needn't handle non-finite values.
Results may differ from a plain program's by a relative error of at most 0.0035.
Values may be sent and summed in bfloat16 or wider, within the bound.
A program may use at most 64 MiB of HBM per device.

v0:
```python
import jax
import numpy as np
import jax.numpy as jnp
from jax import lax
from jax.sharding import PartitionSpec as P


def with_halo(cells, sides, width):
    for axis, dim in sides:
        count = lax.axis_size(axis)
        ends = count - 1
        head = lax.slice_in_dim(cells, 0, width, axis=dim)
        tail = lax.slice_in_dim(cells, cells.shape[dim] - width, cells.shape[dim], axis=dim)
        cells = jnp.concatenate(
            [
                lax.ppermute(tail, axis, [(i, (i + 1) % count) for i in range(ends)]),
                cells,
                lax.ppermute(head, axis, [((i + 1) % count, i) for i in range(ends)]),
            ],
            axis=dim,
        )
    return cells


def tree_gather(block, axis, order):
    count = lax.axis_size(axis)
    me = lax.axis_index(axis)
    held = block
    for dist in order:
        other = lax.ppermute(held, axis, [(i, i ^ dist) for i in range(count)])
        high = me // dist % 2
        size = held.shape[0]
        both = jnp.zeros((2 * size,) + held.shape[1:], held.dtype)
        both = lax.dynamic_update_slice_in_dim(both, held, high * size, 0)
        held = lax.dynamic_update_slice_in_dim(both, other, (1 - high) * size, 0)
    return held


def gather_position(order, count):
    return np.array(
        [sum((j // dist % 2 << k for k, dist in enumerate(order))) for j in range(count)], np.int32
    )


def tree_sum(block, axis, rider):
    count = lax.axis_size(axis)
    me = lax.axis_index(axis)
    order = [1 << k for k in range(count.bit_length() - 1)]
    held = block
    for dist in order:
        half = held.shape[0] // 2
        high = me // dist % 2
        keep = lax.dynamic_slice_in_dim(held, high * half, half, 0)
        send = lax.dynamic_slice_in_dim(held, (1 - high) * half, half, 0)
        held = keep + lax.ppermute(send, axis, [(i, i ^ dist) for i in range(count)])
    chunk = held.shape[0]
    both = tree_gather(jnp.concatenate([held, rider], axis=0), axis, order[::-1])
    both = both.reshape(count, chunk + rider.shape[0], *held.shape[1:])
    return (both[:, :chunk].reshape(count * chunk, *held.shape[1:]), both[:, chunk:])


def swish(value):
    return value * jax.nn.sigmoid(value)


def swish_slope(value):
    sigma = jax.nn.sigmoid(value)
    return sigma * (1.0 + value * (1.0 - sigma))


def convolve(padded, weight, row_count, col_count):
    channels = padded.shape[-1]
    running = None
    for shift_row in range(3):
        for shift_col in range(3):
            window = padded[
                shift_row : shift_row + row_count, shift_col : shift_col + col_count
            ].reshape(row_count * col_count, channels)
            partial_term = jnp.dot(
                window, weight[shift_row, shift_col], preferred_element_type=jnp.float32
            )
            running = partial_term if running is None else running + partial_term
    return running.reshape(row_count, col_count, weight.shape[-1])


def pool_pairs(hidden):
    row_count, col_count, channels = hidden.shape
    return (
        hidden.reshape(row_count // 2, 2, col_count // 2, 2, channels)
        .mean(axis=(1, 3))
        .astype(jnp.bfloat16)
    )


def body(
    section_input, conv_weight, conv_bias, deep_weight, deep_bias, labels, slot_ids, embed_grad
):
    chan_count = lax.axis_size("chan")
    chan_pos = lax.axis_index("chan")
    strip_count = lax.axis_size("strip")
    strip_pos = lax.axis_index("strip")
    row_total, col_local, channels = section_input.shape
    row_part = row_total // chan_count
    half_cols = col_local // 2
    list_len = slot_ids.shape[0]
    owned, width_deep = embed_grad.shape
    lanes = embed_grad.shape[1]
    flat_labels = labels.reshape(-1)
    member = flat_labels[None, :] == jnp.arange(list_len, dtype=jnp.int32)[:, None]
    part_counts = jnp.sum(member.astype(jnp.float32), axis=1)
    meta = jnp.zeros((8, lanes), jnp.float32)
    meta = meta.at[0, :list_len].set(part_counts)
    meta = meta.at[0, list_len : 2 * list_len].set(slot_ids.astype(jnp.float32))
    packed = jnp.concatenate([embed_grad, meta], axis=0)
    order = [strip_count >> k + 1 for k in range(strip_count.bit_length() - 1)]
    position = jnp.asarray(gather_position(order, strip_count))
    early = tree_gather(packed, "strip", order[:2])
    padded_rows = jnp.pad(section_input, ((1, 1), (0, 0), (0, 0)))
    own_rows = lax.dynamic_slice_in_dim(padded_rows, chan_pos * row_part, row_part + 2, 0)
    extended = with_halo(own_rows, (("strip", 1),), 3)
    extended, early = lax.optimization_barrier((extended, early))
    early = tree_gather(early, "strip", order[2:4])
    hidden = swish(convolve(extended, conv_weight, row_part, col_local + 4) + conv_bias)
    pooled = pool_pairs(hidden)
    column = jnp.arange(half_cols + 2)
    outside = (column == 0) & (strip_pos == 0) | (column == half_cols + 1) & (
        strip_pos == strip_count - 1
    )
    pooled = jnp.where(outside[None, :, None], jnp.zeros_like(pooled), pooled)
    pooled, early = lax.optimization_barrier((pooled, early))
    every = tree_gather(early, "strip", order[4:]).reshape(strip_count, owned + 8, lanes)
    every_grad = every[:, :owned].reshape(strip_count * owned, lanes)
    every_counts = every[:, owned, :list_len].reshape(-1)
    every_slots = jnp.round(every[:, owned, list_len : 2 * list_len]).astype(jnp.int32).reshape(-1)
    gathered = lax.all_gather(pooled, "chan", axis=0, tiled=True)
    padded_deep = jnp.pad(gathered, ((1, 1), (0, 0), (0, 0)))
    half_rows = gathered.shape[0]
    deep_pre = convolve(padded_deep, deep_weight, half_rows, half_cols) + deep_bias
    features = swish(deep_pre).astype(jnp.bfloat16).reshape(-1, width_deep)
    part_sums = jnp.dot(member.astype(jnp.bfloat16), features, preferred_element_type=jnp.float32)
    same_slot = (slot_ids[:, None] == every_slots[None, :]).astype(jnp.float32)
    entry_counts = jnp.dot(same_slot, every_counts, precision=lax.Precision.HIGHEST)
    grad_row = position[slot_ids // owned] * owned + slot_ids % owned
    entry_grad = every_grad[grad_row] / jnp.maximum(entry_counts, 1.0)[:, None]
    pixel_grad = lax.dot_general(
        member.astype(jnp.float32),
        entry_grad,
        (((0,), (0,)), ((), ())),
        precision=lax.Precision.HIGHEST,
        preferred_element_type=jnp.float32,
    )
    deep_grad = (pixel_grad * swish_slope(deep_pre.reshape(-1, width_deep))).astype(jnp.bfloat16)
    pieces = []
    for shift_row in range(3):
        for shift_col in range(3):
            window = padded_deep[
                shift_row : shift_row + half_rows, shift_col : shift_col + half_cols
            ].reshape(-1, channels)
            pieces.append(
                lax.dot_general(
                    window, deep_grad, (((0,), (0,)), ((), ())), preferred_element_type=jnp.float32
                )
            )
    local_bias = jnp.sum(deep_grad.astype(jnp.float32), axis=0)
    bias_rows = jnp.zeros((strip_count, width_deep), jnp.float32).at[0].set(local_bias)
    local_grads = jnp.concatenate(pieces + [bias_rows], axis=0)
    total_grads, every_sums = tree_sum(local_grads, "strip", part_sums)
    every_sums = every_sums.reshape(-1, width_deep)
    mine = strip_pos * owned + jnp.arange(owned, dtype=jnp.int32)
    pick = (mine[:, None] == every_slots[None, :]).astype(jnp.float32)
    slot_sums = jnp.dot(pick, every_sums, precision=lax.Precision.HIGHEST)
    slot_counts = jnp.dot(pick, every_counts, precision=lax.Precision.HIGHEST)
    embeddings = slot_sums / jnp.maximum(slot_counts, 1.0)[:, None]
    weight_grad = total_grads[: 9 * channels].reshape(3, 3, channels, width_deep)
    bias_grad = total_grads[9 * channels]
    return (embeddings, weight_grad, bias_grad)


def solution(mesh):
    placed = (
        P(None, "strip", None),
        P(),
        P(),
        P(None, None, None, "chan"),
        P("chan"),
        P(None, "strip"),
        P("strip"),
        P("strip", "chan"),
    )
    return jax.shard_map(
        body,
        mesh=mesh,
        in_specs=placed,
        out_specs=(P("strip", "chan"), P(None, None, None, "chan"), P("chan")),
        check_vma=False,
    )
```

profile of v0, /device:TPU:1, one launch (start us, length us, event | category | flops | bytes accessed | tf_op | source)
XLA Modules:
  0.0 212.5 jit_solution(15142694964070461759)
XLA Ops:
  3.5 2.7 %broadcast_select_fusion = f32[1,32]{1,0:T(1,128)S(1)} fusion(pred[]{:T(512)} %and_reduce_fusion, s32[]{:T(128)} %bitcast.2, s32[]{:T(128)} %bitcast.3, f32[1,32]{1,0:T(1,128)S(1)} %bitcast.147, s32[32]{0:T(128)} %param.21), kind=kLoop, calls=%fused_computation.155 | loop fusion | flops 64 | bytes 393 | tf_op jit(solution)/shard_map/select.4
  8.5 3.6 %collective-permute-start.2 = (f32[72,128]{1,0:T(8,128)S(1)}, f32[72,128]{1,0:T(8,128)S(1)}, u32[]{:S(2)}, u32[]{:S(2)}) collective-permute-start(f32[72,128]{1,0:T(8,128)S(1)} %get-tuple-element.67), channel_id=1, source_target_pairs={{0,128},{4,132},{8,136},{12,140},{16,144},{20,148},{24,152},{28,15... | collective-permute-start | bytes 110600 | tf_op jit(solution)/shard_map/ppermute | solution.py:30
  13.1 4.4 %collective-permute-start = (bf16[14,3,256]{2,1,0:T(4,128)(2,1)S(1)}, bf16[14,3,256]{2,1,0:T(4,128)(2,1)S(1)}, u32[]{:S(2)}, u32[]{:S(2)}) collective-permute-start(bf16[14,3,256]{2,1,0:T(4,128)(2,1)S(1)} %get-tuple-element.47), channel_id=1, source_target_pairs={{0,4},{4,8},{8,12},{12,16},{16,20},{20,24},{24,28},{28,32},{32,36}... | collective-permute-start | bytes 64520 | tf_op jit(solution)/shard_map/ppermute | solution.py:16
  20.6 2.2 %collective-permute-done.1 = bf16[14,3,256]{2,1,0:T(4,128)(2,1)S(1)} collective-permute-done((bf16[14,3,256]{2,1,0:T(4,128)(2,1)S(1)}, bf16[14,3,256]{2,1,0:T(4,128)(2,1)S(1)}, u32[]{:S(2)}, u32[]{:S(2)}) %collective-permute-start.1) | collective-permute-done | bytes 21536 | tf_op jit(solution)/shard_map/ppermute | solution.py:18
  23.9 2.6 %collective-permute-done.3 = f32[144,128]{1,0:T(8,128)S(1)} collective-permute-done((f32[144,128]{1,0:T(8,128)S(1)}, f32[144,128]{1,0:T(8,128)S(1)}, u32[]{:S(2)}, u32[]{:S(2)}) %collective-permute-start.3) | collective-permute-done | bytes 73760 | tf_op jit(solution)/shard_map/ppermute | solution.py:30
  26.5 6.3 %collective-permute-start.4 = (f32[288,128]{1,0:T(8,128)S(1)}, f32[288,128]{1,0:T(8,128)}, u32[]{:S(2)}, u32[]{:S(2)}) collective-permute-start(f32[288,128]{1,0:T(8,128)S(1)} %constant_dynamic-update-slice_fusion.14), channel_id=1, source_target_pairs={{0,32},{4,36},{8,40},{12,44},{16,48},{20,52},{24,56},{28,60},{32,0... | collective-permute-start | bytes 442376 | tf_op jit(solution)/shard_map/ppermute | solution.py:30
  32.8 2.5 %fusion.62 = (bf16[12,132,256]{2,1,0:T(8,128)(2,1)S(1)}, bf16[12,132,256]{2,1,0:T(8,128)(2,1)S(1)}, bf16[12,132,256]{2,1,0:T(8,128)(2,1)S(1)}, bf16[12,132,256]{...) fusion(bf16[14,134,256]{2,1,0:T(8,128)(2,1)S(1)} %pad_maximum_f, ...), kind=kLoop, calls=%fused_computation.161 | loop fusion | bytes 14598144 | tf_op jit(solution)/shard_map/slice | solution.py:76
  35.3 2.0 reshape.215
  37.3 2.1 reshape.216
  41.4 2.1 reshape.218
  43.5 2.0 reshape.219
  59.0 2.7 %fusion.2 = f32[6,66,256]{2,1,0:T(8,128)S(1)} fusion(f32[6,2,66,2,256]{4,3,2,1,0:T(2,128)S(1)} %reshape.224, f32[256]{0:T(256)S(1)} %copy-done.24), kind=kLoop, calls=%fused_computation.25 | loop fusion | flops 2331648 | bytes 2028544 | tf_op jit(solution)/shard_map/reduce_sum | solution.py:90
  62.7 2.1 collective-permute-start.5
  64.9 12.7 %collective-permute-done.5 = f32[576,128]{1,0:T(8,128)S(1)} collective-permute-done((f32[576,128]{1,0:T(8,128)S(1)}, f32[576,128]{1,0:T(8,128)S(1)}, u32[]{:S(2)}, u32[]{:S(2)}) %collective-permute-start.5) | collective-permute-done | bytes 294944 | tf_op jit(solution)/shard_map/ppermute | solution.py:30
  78.0 12.9 %all_gather.3 = bf16[24,66,256]{2,1,0:T(8,128)(2,1)S(1)} all-gather(bf16[6,66,256]{2,1,0:T(8,128)(2,1)S(1)} %fusion.13), channel_id=1, replica_groups=mesh['strip'=64,'chan'=4] {'chan'}, dimensions={0}, use_global_device_ids=true | all-gather | bytes 1013760 | tf_op jit(solution)/shard_map/all_gather | solution.py:135
  95.4 3.7 %collective-permute-start.7 = (f32[2304,128]{1,0:T(8,128)S(1)}, f32[2304,128]{1,0:T(8,128)S(1)}, u32[]{:S(2)}, u32[]{:S(2)}) collective-permute-start(f32[2304,128]{1,0:T(8,128)S(1)} %constant_dynamic-update-slice_fusion.8), channel_id=1, source_target_pairs={{0,4},{4,0},{8,12},{12,8},{16,20},{20,16},{24,28},{28,24},{32,36},... | collective-permute-start | bytes 3538952 | tf_op jit(solution)/shard_map/ppermute | solution.py:30
  104.0 2.2 %gather_fusion.1 = f32[32,128]{1,0:T(8,128)S(1)} fusion(f32[4096,128]{1,0:T(8,128)} %bitcast.144, s32[1024]{0:T(1024)S(1)} %pad_clamp_fusion), kind=kCustom, calls=%fused_computation.1 | custom fusion | bytes 32896 | tf_op jit(solution)/shard_map/gather | solution.py:144
  106.2 2.1 convert_reduce_fusion
  119.3 7.3 %collective-permute-done.9 = f32[592,128]{1,0:T(8,128)S(1)} collective-permute-done((f32[592,128]{1,0:T(8,128)S(1)}, f32[592,128]{1,0:T(8,128)S(1)}, u32[]{:S(2)}, u32[]{:S(2)}) %collective-permute-start.9) | collective-permute-done | bytes 303136 | tf_op jit(solution)/shard_map/ppermute | solution.py:55
  126.6 2.2 %collective-permute-start.10 = (f32[296,128]{1,0:T(8,128)S(1)}, f32[296,128]{1,0:T(8,128)S(1)}, u32[]{:S(2)}, u32[]{:S(2)}) collective-permute-start(f32[296,128]{1,0:T(8,128)S(1)} %constant_dynamic-slice_fusion.3), channel_id=1, source_target_pairs={{0,16},{4,20},{8,24},{12,28},{16,0},{20,4},{24,8},{28,12},{32,48},... | collective-permute-start | bytes 454664 | tf_op jit(solution)/shard_map/ppermute | solution.py:55
  128.8 6.9 %collective-permute-done.10 = f32[296,128]{1,0:T(8,128)S(1)} collective-permute-done((f32[296,128]{1,0:T(8,128)S(1)}, f32[296,128]{1,0:T(8,128)S(1)}, u32[]{:S(2)}, u32[]{:S(2)}) %collective-permute-start.10) | collective-permute-done | bytes 151584 | tf_op jit(solution)/shard_map/ppermute | solution.py:55
  136.2 6.8 %collective-permute-done.11 = f32[148,128]{1,0:T(8,128)S(1)} collective-permute-done((f32[148,128]{1,0:T(8,128)S(1)}, f32[148,128]{1,0:T(8,128)S(1)}, u32[]{:S(2)}, u32[]{:S(2)}) %collective-permute-start.11) | collective-permute-done | bytes 75808 | tf_op jit(solution)/shard_map/ppermute | solution.py:55
  143.4 2.5 %collective-permute-done.12 = f32[74,128]{1,0:T(8,128)S(1)} collective-permute-done((f32[74,128]{1,0:T(8,128)S(1)}, f32[74,128]{1,0:T(8,128)S(1)}, u32[]{:S(2)}, u32[]{:S(2)}) %collective-permute-start.12) | collective-permute-done | bytes 37920 | tf_op jit(solution)/shard_map/ppermute | solution.py:55
  147.5 3.0 %collective-permute-done.13 = f32[37,128]{1,0:T(8,128)S(1)} collective-permute-done((f32[37,128]{1,0:T(8,128)S(1)}, f32[37,128]{1,0:T(8,128)S(1)}, u32[]{:S(2)}, u32[]{:S(2)}) %collective-permute-start.13) | collective-permute-done | bytes 18976 | tf_op jit(solution)/shard_map/ppermute | solution.py:55
  151.8 3.6 %collective-permute-done.14 = f32[69,128]{1,0:T(8,128)S(1)} collective-permute-done((f32[69,128]{1,0:T(8,128)S(1)}, f32[69,128]{1,0:T(8,128)S(1)}, u32[]{:S(2)}, u32[]{:S(2)}) %collective-permute-start.14) | collective-permute-done | bytes 35360 | tf_op jit(solution)/shard_map/ppermute | solution.py:30
  156.4 2.9 %collective-permute-done.15 = f32[138,128]{1,0:T(8,128)S(1)} collective-permute-done((f32[138,128]{1,0:T(8,128)S(1)}, f32[138,128]{1,0:T(8,128)S(1)}, u32[]{:S(2)}, u32[]{:S(2)}) %collective-permute-start.15) | collective-permute-done | bytes 70688 | tf_op jit(solution)/shard_map/ppermute | solution.py:30
  160.9 6.7 %collective-permute-done.16 = f32[276,128]{1,0:T(8,128)S(1)} collective-permute-done((f32[276,128]{1,0:T(8,128)S(1)}, f32[276,128]{1,0:T(8,128)S(1)}, u32[]{:S(2)}, u32[]{:S(2)}) %collective-permute-start.16) | collective-permute-done | bytes 141344 | tf_op jit(solution)/shard_map/ppermute | solution.py:30
  168.5 11.4 %collective-permute-done.17 = f32[552,128]{1,0:T(8,128)S(1)} collective-permute-done((f32[552,128]{1,0:T(8,128)S(1)}, f32[552,128]{1,0:T(8,128)S(1)}, u32[]{:S(2)}, u32[]{:S(2)}) %collective-permute-start.17) | collective-permute-done | bytes 282656 | tf_op jit(solution)/shard_map/ppermute | solution.py:30
  180.1 12.5 %collective-permute-done.18 = f32[1104,128]{1,0:T(8,128)S(1)} collective-permute-done((f32[1104,128]{1,0:T(8,128)S(1)}, f32[1104,128]{1,0:T(8,128)S(1)}, u32[]{:S(2)}, u32[]{:S(2)}) %collective-permute-start.18) | collective-permute-done | bytes 565280 | tf_op jit(solution)/shard_map/ppermute | solution.py:30
  192.7 5.6 %collective-permute-start.19 = (f32[2208,128]{1,0:T(8,128)S(1)}, f32[2208,128]{1,0:T(8,128)S(1)}, u32[]{:S(2)}, u32[]{:S(2)}) collective-permute-start(f32[2208,128]{1,0:T(8,128)S(1)} %constant_dynamic-update-slice_fusion.2), channel_id=1, source_target_pairs={{0,4},{4,0},{8,12},{12,8},{16,20},{20,16},{24,28},{28,24},{32,36},... | collective-permute-start | bytes 3391496 | tf_op jit(solution)/shard_map/ppermute | solution.py:30
  205.2 2.4 %reshape.239 = f32[2368,128]{1,0:T(8,128)} reshape(f32[64,37,128]{2,1,0:T(8,128)} %slice.257) | data formatting | bytes 2424832 | tf_op jit(solution)/shard_map/reshape | solution.py:59
  207.6 2.4 %slice.258 = f32[2304,128]{1,0:T(8,128)} slice(f32[2368,128]{1,0:T(8,128)} %reshape.239), slice={[0:2304], [0:128]} | slice | bytes 2359296 | tf_op jit(solution)/shard_map/slice | solution.py:174
  (189 shorter events, 64.1 us)
Async XLA Ops:
  8.5 14.6 %collective-permute-start.2 = (f32[72,128]{1,0:T(8,128)S(1)}, f32[72,128]{1,0:T(8,128)S(1)}, u32[]{:S(2)}, u32[]{:S(2)}) collective-permute-start(f32[72,128]{1,0:T(8,128)S(1)} %get-tuple-element.67), channel_id=1, source_target_pairs={{0,128},{4,132},{8,136},{12,140},{16,144},{20,148},{24,152},{28,15... | collective-permute-start | bytes 110600 | tf_op jit(solution)/shard_map/ppermute | solution.py:30
  12.1 7.4 %copy-start.1 = (bf16[48,128,256]{2,1,0:T(8,128)(2,1)S(1)}, bf16[48,128,256]{2,1,0:T(8,128)(2,1)}, u32[]{:S(2)}) copy-start(bf16[48,128,256]{2,1,0:T(8,128)(2,1)} %param.15) | copy-start | bytes 9437188
  13.1 7.4 %collective-permute-start = (bf16[14,3,256]{2,1,0:T(4,128)(2,1)S(1)}, bf16[14,3,256]{2,1,0:T(4,128)(2,1)S(1)}, u32[]{:S(2)}, u32[]{:S(2)}) collective-permute-start(bf16[14,3,256]{2,1,0:T(4,128)(2,1)S(1)} %get-tuple-element.47), channel_id=1, source_target_pairs={{0,4},{4,8},{8,12},{12,16},{16,20},{20,24},{24,28},{28,32},{32,36}... | collective-permute-start | bytes 64520 | tf_op jit(solution)/shard_map/ppermute | solution.py:16
  17.5 2.1 copy-start.25
  17.5 2.1 copy-start
  17.5 5.2 %collective-permute-start.1 = (bf16[14,3,256]{2,1,0:T(4,128)(2,1)S(1)}, bf16[14,3,256]{2,1,0:T(4,128)(2,1)S(1)}, u32[]{:S(2)}, u32[]{:S(2)}) collective-permute-start(bf16[14,3,256]{2,1,0:T(4,128)(2,1)S(1)} %get-tuple-element.48), channel_id=1, source_target_pairs={{4,0},{8,4},{12,8},{16,12},{20,16},{24,20},{28,24},{32,28},{36,32}... | collective-permute-start | bytes 64520 | tf_op jit(solution)/shard_map/ppermute | solution.py:18
  23.2 3.3 %collective-permute-start.3 = (f32[144,128]{1,0:T(8,128)S(1)}, f32[144,128]{1,0:T(8,128)S(1)}, u32[]{:S(2)}, u32[]{:S(2)}) collective-permute-start(f32[144,128]{1,0:T(8,128)S(1)} %constant_dynamic-update-slice_fusion.16), channel_id=1, source_target_pairs={{0,64},{4,68},{8,72},{12,76},{16,80},{20,84},{24,88},{28,92},{32,9... | collective-permute-start | bytes 221192 | tf_op jit(solution)/shard_map/ppermute | solution.py:30
  26.5 35.3 %collective-permute-start.4 = (f32[288,128]{1,0:T(8,128)S(1)}, f32[288,128]{1,0:T(8,128)}, u32[]{:S(2)}, u32[]{:S(2)}) collective-permute-start(f32[288,128]{1,0:T(8,128)S(1)} %constant_dynamic-update-slice_fusion.14), channel_id=1, source_target_pairs={{0,32},{4,36},{8,40},{12,44},{16,48},{20,52},{24,56},{28,60},{32,0... | collective-permute-start | bytes 442376 | tf_op jit(solution)/shard_map/ppermute | solution.py:30
  48.8 1.4 copy-start.19
  48.8 1.6 copy-start.21
  62.7 14.9 %collective-permute-start.5 = (f32[576,128]{1,0:T(8,128)S(1)}, f32[576,128]{1,0:T(8,128)S(1)}, u32[]{:S(2)}, u32[]{:S(2)}) collective-permute-start(f32[576,128]{1,0:T(8,128)S(1)} %constant_dynamic-update-slice_fusion.12), channel_id=1, source_target_pairs={{0,16},{4,20},{8,24},{12,28},{16,0},{20,4},{24,8},{28,12},{32,48},... | collective-permute-start | bytes 884744 | tf_op jit(solution)/shard_map/ppermute | solution.py:30
  77.7 17.6 %collective-permute-start.6 = (f32[1152,128]{1,0:T(8,128)S(1)}, f32[1152,128]{1,0:T(8,128)S(1)}, u32[]{:S(2)}, u32[]{:S(2)}) collective-permute-start(f32[1152,128]{1,0:T(8,128)S(1)} %constant_dynamic-update-slice_fusion.10), channel_id=1, source_target_pairs={{0,8},{4,12},{8,0},{12,4},{16,24},{20,28},{24,16},{28,20},{32,40},... | collective-permute-start | bytes 1769480 | tf_op jit(solution)/shard_map/ppermute | solution.py:30
  90.8 1.4 copy-start.23
  92.3 1.4 copy-start.6
  92.3 1.8 copy-start.4
  92.3 2.3 %copy-start.2 = (bf16[24,64,256]{2,1,0:T(8,128)(2,1)}, bf16[24,64,256]{2,1,0:T(8,128)(2,1)S(1)}, u32[]{:S(2)}) copy-start(bf16[24,64,256]{2,1,0:T(8,128)(2,1)S(1)} %get-tuple-element.64) | copy-start | bytes 2359300
  95.4 6.2 %collective-permute-start.7 = (f32[2304,128]{1,0:T(8,128)S(1)}, f32[2304,128]{1,0:T(8,128)S(1)}, u32[]{:S(2)}, u32[]{:S(2)}) collective-permute-start(f32[2304,128]{1,0:T(8,128)S(1)} %constant_dynamic-update-slice_fusion.8), channel_id=1, source_target_pairs={{0,4},{4,0},{8,12},{12,8},{16,20},{20,16},{24,28},{28,24},{32,36},... | collective-permute-start | bytes 3538952 | tf_op jit(solution)/shard_map/ppermute | solution.py:30
  106.2 2.1 copy-start.11
  108.3 1.5 copy-start.7
  114.2 2.1 collective-permute-start.8
  117.5 29.7 %copy-start.22 = (f32[1536,128]{1,0:T(8,128)S(1)}, f32[1536,128]{1,0:T(8,128)}, u32[]{:S(2)}) copy-start(f32[1536,128]{1,0:T(8,128)} %fusion) | copy-start | bytes 2359300
  117.5 9.0 %collective-permute-start.9 = (f32[592,128]{1,0:T(8,128)S(1)}, f32[592,128]{1,0:T(8,128)S(1)}, u32[]{:S(2)}, u32[]{:S(2)}) collective-permute-start(f32[592,128]{1,0:T(8,128)S(1)} %constant_dynamic-slice_fusion.4), channel_id=1, source_target_pairs={{0,8},{4,12},{8,0},{12,4},{16,24},{20,28},{24,16},{28,20},{32,40},... | collective-permute-start | bytes 909320 | tf_op jit(solution)/shard_map/ppermute | solution.py:55
  126.6 9.1 %collective-permute-start.10 = (f32[296,128]{1,0:T(8,128)S(1)}, f32[296,128]{1,0:T(8,128)S(1)}, u32[]{:S(2)}, u32[]{:S(2)}) collective-permute-start(f32[296,128]{1,0:T(8,128)S(1)} %constant_dynamic-slice_fusion.3), channel_id=1, source_target_pairs={{0,16},{4,20},{8,24},{12,28},{16,0},{20,4},{24,8},{28,12},{32,48},... | collective-permute-start | bytes 454664 | tf_op jit(solution)/shard_map/ppermute | solution.py:55
  135.8 7.2 %collective-permute-start.11 = (f32[148,128]{1,0:T(8,128)S(1)}, f32[148,128]{1,0:T(8,128)S(1)}, u32[]{:S(2)}, u32[]{:S(2)}) collective-permute-start(f32[148,128]{1,0:T(8,128)S(1)} %constant_dynamic-slice_fusion.2), channel_id=1, source_target_pairs={{0,32},{4,36},{8,40},{12,44},{16,48},{20,52},{24,56},{28,60},{32,0... | collective-permute-start | bytes 227336 | tf_op jit(solution)/shard_map/ppermute | solution.py:55
  143.0 2.9 %collective-permute-start.12 = (f32[74,128]{1,0:T(8,128)S(1)}, f32[74,128]{1,0:T(8,128)S(1)}, u32[]{:S(2)}, u32[]{:S(2)}) collective-permute-start(f32[74,128]{1,0:T(8,128)S(1)} %constant_dynamic-slice_fusion.1), channel_id=1, source_target_pairs={{0,64},{4,68},{8,72},{12,76},{16,80},{20,84},{24,88},{28,92},{32,9... | collective-permute-start | bytes 113672 | tf_op jit(solution)/shard_map/ppermute | solution.py:55
  146.0 4.5 %collective-permute-start.13 = (f32[37,128]{1,0:T(8,128)S(1)}, f32[37,128]{1,0:T(8,128)S(1)}, u32[]{:S(2)}, u32[]{:S(2)}) collective-permute-start(f32[37,128]{1,0:T(8,128)S(1)} %constant_dynamic-slice_fusion), channel_id=1, source_target_pairs={{0,128},{4,132},{8,136},{12,140},{16,144},{20,148},{24,152},{28,15... | collective-permute-start | bytes 56840 | tf_op jit(solution)/shard_map/ppermute | solution.py:55
  150.5 4.9 %collective-permute-start.14 = (f32[69,128]{1,0:T(8,128)S(1)}, f32[69,128]{1,0:T(8,128)S(1)}, u32[]{:S(2)}, u32[]{:S(2)}) collective-permute-start(f32[69,128]{1,0:T(8,128)S(1)} %pad_maximum_fusion.2), channel_id=1, source_target_pairs={{0,128},{4,132},{8,136},{12,140},{16,144},{20,148},{24,152},{28,15... | collective-permute-start | bytes 105992 | tf_op jit(solution)/shard_map/ppermute | solution.py:30
  155.6 3.7 %collective-permute-start.15 = (f32[138,128]{1,0:T(8,128)S(1)}, f32[138,128]{1,0:T(8,128)S(1)}, u32[]{:S(2)}, u32[]{:S(2)}) collective-permute-start(f32[138,128]{1,0:T(8,128)S(1)} %dynamic_update_slice.85), channel_id=1, source_target_pairs={{0,64},{4,68},{8,72},{12,76},{16,80},{20,84},{24,88},{28,92},{32,9... | collective-permute-start | bytes 211976 | tf_op jit(solution)/shard_map/ppermute | solution.py:30
  159.7 7.9 %collective-permute-start.16 = (f32[276,128]{1,0:T(8,128)S(1)}, f32[276,128]{1,0:T(8,128)S(1)}, u32[]{:S(2)}, u32[]{:S(2)}) collective-permute-start(f32[276,128]{1,0:T(8,128)S(1)} %dynamic_update_slice.87), channel_id=1, source_target_pairs={{0,32},{4,36},{8,40},{12,44},{16,48},{20,52},{24,56},{28,60},{32,0... | collective-permute-start | bytes 423944 | tf_op jit(solution)/shard_map/ppermute | solution.py:30
  168.3 11.6 %collective-permute-start.17 = (f32[552,128]{1,0:T(8,128)S(1)}, f32[552,128]{1,0:T(8,128)S(1)}, u32[]{:S(2)}, u32[]{:S(2)}) collective-permute-start(f32[552,128]{1,0:T(8,128)S(1)} %dynamic_update_slice.89), channel_id=1, source_target_pairs={{0,16},{4,20},{8,24},{12,28},{16,0},{20,4},{24,8},{28,12},{32,48},... | collective-permute-start | bytes 847880 | tf_op jit(solution)/shard_map/ppermute | solution.py:30
  179.9 12.8 %collective-permute-start.18 = (f32[1104,128]{1,0:T(8,128)S(1)}, f32[1104,128]{1,0:T(8,128)S(1)}, u32[]{:S(2)}, u32[]{:S(2)}) collective-permute-start(f32[1104,128]{1,0:T(8,128)S(1)} %constant_dynamic-update-slice_fusion.4), channel_id=1, source_target_pairs={{0,8},{4,12},{8,0},{12,4},{16,24},{20,28},{24,16},{28,20},{32,40},... | collective-permute-start | bytes 1695752 | tf_op jit(solution)/shard_map/ppermute | solution.py:30
  192.7 8.6 %collective-permute-start.19 = (f32[2208,128]{1,0:T(8,128)S(1)}, f32[2208,128]{1,0:T(8,128)S(1)}, u32[]{:S(2)}, u32[]{:S(2)}) collective-permute-start(f32[2208,128]{1,0:T(8,128)S(1)} %constant_dynamic-update-slice_fusion.2), channel_id=1, source_target_pairs={{0,4},{4,0},{8,12},{12,8},{16,20},{20,16},{24,28},{28,24},{32,36},... | collective-permute-start | bytes 3391496 | tf_op jit(solution)/shard_map/ppermute | solution.py:30
  (15 other events, 16.3 us)
where the time goes:
time: 213 us; the launch traced here: 212 us
  waiting for transfers between devices  82.6 us (39%)
  local copies, waits for them, and re-layouts  53 us (25%)
  starting transfers between devices  36.2 us (17%)
  matrix products  16.5 us (8%)
  blocking collectives  12.9 us (6%)
  other arithmetic  9.54 us (4%)
    ppermute x12, waiting for transfers between devices, tree_gather(): other = lax.ppermute(held, axis, [(i, i ^ dist) for i in range(count)])  52.3 us
    ppermute x6, waiting for transfers between devices, tree_sum(): lax.ppermute(send, axis, [(i, i ^ dist) for i in range(count)])  28.2 us
    ppermute x12, starting transfers between devices, tree_gather(): other = lax.ppermute(held, axis, [(i, i ^ dist) for i in range(count)])  23.5 us
    reshape x9, local copies, waits for them, and re-layouts, convolve(): window = padded[shift_row:shift_row + row_count, shift_col:shift_col + co...  13.5 us
    all_gather x1, blocking collectives, body(): gathered = lax.all_gather(pooled, 'chan', axis=0, tiled=True)  12.9 us
    dot_general x18, matrix products, convolve(): jnp.dot(window, weight[shift_row, shift_col], preferred_element_type=jnp....  8.6 us
    unnamed x54, local copies, waits for them, and re-layouts  7.77 us
    ppermute x6, starting transfers between devices, tree_sum(): lax.ppermute(send, axis, [(i, i ^ dist) for i in range(count)])  6.37 us
  transfers between devices with their start and end apart: 20, of which 14 were waited for; matrix products, arithmetic and copies ran while one was open for 18% of the time, Pallas kernels for 0%

commit v1 on v0

--- a/solution.py
+++ b/solution.py
@@ -132,7 +132,12 @@
     every_grad = every[:, :owned].reshape(strip_count * owned, lanes)
     every_counts = every[:, owned, :list_len].reshape(-1)
     every_slots = jnp.round(every[:, owned, list_len : 2 * list_len]).astype(jnp.int32).reshape(-1)
-    gathered = lax.all_gather(pooled, "chan", axis=0, tiled=True)
+    gathered = jnp.concatenate(
+        jax.lax.all_to_all(
+            jnp.stack(tuple((pooled for _ in range(jax.lax.axis_size("chan"))))), "chan", 0, 0
+        ),
+        axis=0,
+    )
     padded_deep = jnp.pad(gathered, ((1, 1), (0, 0), (0, 0)))
     half_rows = gathered.shape[0]
     deep_pre = convolve(padded_deep, deep_weight, half_rows, half_cols) + deep_bias

time: 213 us -> 216 us (1.014)
  blocking collectives: 12.9 us -> 0 us
  starting transfers between devices: 36.2 us -> 44.2 us
  local copies, waits for them, and re-layouts: 53 us -> 59.1 us
  waiting for transfers between devices: 82.6 us -> 86.2 us
  matrix products: 16.5 us -> 14.3 us
    all_gather x1 -> x0, blocking collectives: 12.9 us -> none  [body(): gathered = lax.all_gather(pooled, 'chan', axis=0, tiled=True)]
    all_to_all x0 -> x1, starting transfers between devices: none -> 4.17 us  [body(): jax.lax.all_to_all(jnp.stack(tuple((pooled for _ in range(jax.lax.axis_si...]
    ppermute x6, starting transfers between devices: 6.37 us -> 9.42 us  [tree_sum(): lax.ppermute(send, axis, [(i, i ^ dist) for i in range(count)])]
    ppermute x12, waiting for transfers between devices: 52.3 us -> 54.5 us  [tree_gather(): other = lax.ppermute(held, axis, [(i, i ^ dist) for i in range(count)])]
    unnamed x54 -> x66, local copies, waits for them, and re-layouts: 7.77 us -> 7.39 us
  transfers between devices with their start and end apart: 20 -> 21, of which waited for: 14 -> 15; matrix products, arithmetic and copies ran while one was open for 18% -> 20% of each run, Pallas kernels for 0% -> 0%
where the time goes in v1:
time: 216 us; the launch traced here: 215 us
  waiting for transfers between devices  86.2 us (40%)
  local copies, waits for them, and re-layouts  59.1 us (27%)
  starting transfers between devices  44.2 us (20%)
  matrix products  14.3 us (7%)
  other arithmetic  9.54 us (4%)
    ppermute x12, waiting for transfers between devices, tree_gather(): other = lax.ppermute(held, axis, [(i, i ^ dist) for i in range(count)])  54.5 us
    ppermute x6, waiting for transfers between devices, tree_sum(): lax.ppermute(send, axis, [(i, i ^ dist) for i in range(count)])  28.8 us
    ppermute x12, starting transfers between devices, tree_gather(): other = lax.ppermute(held, axis, [(i, i ^ dist) for i in range(count)])  24.3 us
    reshape x9, local copies, waits for them, and re-layouts, convolve(): window = padded[shift_row:shift_row + row_count, shift_col:shift_col + co...  13.6 us
    ppermute x6, starting transfers between devices, tree_sum(): lax.ppermute(send, axis, [(i, i ^ dist) for i in range(count)])  9.42 us
    dot_general x18, matrix products, convolve(): jnp.dot(window, weight[shift_row, shift_col], preferred_element_type=jnp....  7.7 us
    unnamed x66, local copies, waits for them, and re-layouts  7.39 us
    dynamic_update_slice x12, local copies, waits for them, and re-layouts, tree_gather(): held = lax.dynamic_update_slice_in_dim(both, other, (1 - high) * size, 0)  5.57 us
  transfers between devices with their start and end apart: 21, of which 15 were waited for; matrix products, arithmetic and copies ran while one was open for 20% of the time, Pallas kernels for 0%

profile of v1, /device:TPU:1, one launch (start us, length us, event | category | flops | bytes accessed | tf_op | source)
XLA Modules:
  0.0 215.2 jit_solution(2696807104057699736)
XLA Ops:
  3.5 2.7 %broadcast_select_fusion = f32[1,32]{1,0:T(1,128)S(1)} fusion(pred[]{:T(512)} %and_reduce_fusion, s32[]{:T(128)} %bitcast.2, s32[]{:T(128)} %bitcast.3, f32[1,32]{1,0:T(1,128)S(1)} %bitcast.149, s32[32]{0:T(128)} %param.21), kind=kLoop, calls=%fused_computation.155 | loop fusion | flops 64 | bytes 393 | tf_op jit(solution)/shard_map/select.4
  8.5 3.6 %collective-permute-start.2 = (f32[72,128]{1,0:T(8,128)S(1)}, f32[72,128]{1,0:T(8,128)S(1)}, u32[]{:S(2)}, u32[]{:S(2)}) collective-permute-start(f32[72,128]{1,0:T(8,128)S(1)} %get-tuple-element.67), channel_id=1, source_target_pairs={{0,128},{4,132},{8,136},{12,140},{16,144},{20,148},{24,152},{28,15... | collective-permute-start | bytes 110600 | tf_op jit(solution)/shard_map/ppermute | solution.py:30
  13.1 4.4 %collective-permute-start = (bf16[14,3,256]{2,1,0:T(4,128)(2,1)S(1)}, bf16[14,3,256]{2,1,0:T(4,128)(2,1)S(1)}, u32[]{:S(2)}, u32[]{:S(2)}) collective-permute-start(bf16[14,3,256]{2,1,0:T(4,128)(2,1)S(1)} %get-tuple-element.47), channel_id=1, source_target_pairs={{0,4},{4,8},{8,12},{12,16},{16,20},{20,24},{24,28},{28,32},{32,36}... | collective-permute-start | bytes 64520 | tf_op jit(solution)/shard_map/ppermute | solution.py:16
  19.7 3.0 %collective-permute-done.1 = bf16[14,3,256]{2,1,0:T(4,128)(2,1)S(1)} collective-permute-done((bf16[14,3,256]{2,1,0:T(4,128)(2,1)S(1)}, bf16[14,3,256]{2,1,0:T(4,128)(2,1)S(1)}, u32[]{:S(2)}, u32[]{:S(2)}) %collective-permute-start.1) | collective-permute-done | bytes 21536 | tf_op jit(solution)/shard_map/ppermute | solution.py:18
  23.9 2.6 %collective-permute-done.3 = f32[144,128]{1,0:T(8,128)S(1)} collective-permute-done((f32[144,128]{1,0:T(8,128)S(1)}, f32[144,128]{1,0:T(8,128)S(1)}, u32[]{:S(2)}, u32[]{:S(2)}) %collective-permute-start.3) | collective-permute-done | bytes 73760 | tf_op jit(solution)/shard_map/ppermute | solution.py:30
  26.5 6.1 %collective-permute-start.4 = (f32[288,128]{1,0:T(8,128)S(1)}, f32[288,128]{1,0:T(8,128)}, u32[]{:S(2)}, u32[]{:S(2)}) collective-permute-start(f32[288,128]{1,0:T(8,128)S(1)} %constant_dynamic-update-slice_fusion.14), channel_id=1, source_target_pairs={{0,32},{4,36},{8,40},{12,44},{16,48},{20,52},{24,56},{28,60},{32,0... | collective-permute-start | bytes 442376 | tf_op jit(solution)/shard_map/ppermute | solution.py:30
  32.6 2.5 %fusion.62 = (bf16[12,132,256]{2,1,0:T(8,128)(2,1)S(1)}, bf16[12,132,256]{2,1,0:T(8,128)(2,1)S(1)}, bf16[12,132,256]{2,1,0:T(8,128)(2,1)S(1)}, bf16[12,132,256]{...) fusion(bf16[14,134,256]{2,1,0:T(8,128)(2,1)S(1)} %pad_maximum_f, ...), kind=kLoop, calls=%fused_computation.161 | loop fusion | bytes 14598144 | tf_op jit(solution)/shard_map/slice | solution.py:76
  35.1 2.1 reshape.220
  39.2 2.1 reshape.222
  41.3 2.1 reshape.223
  58.9 2.7 %fusion.2 = f32[6,66,256]{2,1,0:T(8,128)S(1)} fusion(f32[6,2,66,2,256]{4,3,2,1,0:T(2,128)S(1)} %reshape.229, f32[256]{0:T(256)S(1)} %copy-done.30), kind=kLoop, calls=%fused_computation.25 | loop fusion | flops 2331648 | bytes 2028544 | tf_op jit(solution)/shard_map/reduce_sum | solution.py:90
  62.6 2.2 %collective-permute-start.5 = (f32[576,128]{1,0:T(8,128)S(1)}, f32[576,128]{1,0:T(8,128)S(1)}, u32[]{:S(2)}, u32[]{:S(2)}) collective-permute-start(f32[576,128]{1,0:T(8,128)S(1)} %constant_dynamic-update-slice_fusion.12), channel_id=1, source_target_pairs={{0,16},{4,20},{8,24},{12,28},{16,0},{20,4},{24,8},{28,12},{32,48},... | collective-permute-start | bytes 884744 | tf_op jit(solution)/shard_map/ppermute | solution.py:30
  65.0 12.7 %collective-permute-done.5 = f32[576,128]{1,0:T(8,128)S(1)} collective-permute-done((f32[576,128]{1,0:T(8,128)S(1)}, f32[576,128]{1,0:T(8,128)S(1)}, u32[]{:S(2)}, u32[]{:S(2)}) %collective-permute-start.5) | collective-permute-done | bytes 294944 | tf_op jit(solution)/shard_map/ppermute | solution.py:30
  79.7 4.2 %all-to-all-start = ((bf16[4,6,66,256]{3,2,1,0:T(8,128)(2,1)}), bf16[4,6,66,256]{3,2,1,0:T(8,128)(2,1)S(1)}, u32[]{:S(2)}, u32[]{:S(2)}) async-start(bf16[4,6,66,256]{3,2,1,0:T(8,128)(2,1)} %stack.2), calls=%async_computation | async-start | bytes 1769472 | tf_op jit(solution)/shard_map/all_to_all | solution.py:136
  85.9 5.0 %collective-permute-done.6 = f32[1152,128]{1,0:T(8,128)S(1)} collective-permute-done((f32[1152,128]{1,0:T(8,128)S(1)}, f32[1152,128]{1,0:T(8,128)S(1)}, u32[]{:S(2)}, u32[]{:S(2)}) %collective-permute-start.6) | collective-permute-done | bytes 589856 | tf_op jit(solution)/shard_map/ppermute | solution.py:30
  91.7 2.7 %collective-permute-start.7 = (f32[2304,128]{1,0:T(8,128)}, f32[2304,128]{1,0:T(8,128)}, u32[]{:S(2)}, u32[]{:S(2)}) collective-permute-start(f32[2304,128]{1,0:T(8,128)} %constant_dynamic-update-slice_fusion.8), channel_id=1, source_target_pairs={{0,4},{4,0},{8,12},{12,8},{16,20},{20,16},{24,28},{28,24},{32,36},... | collective-permute-start | bytes 3538952 | tf_op jit(solution)/shard_map/ppermute | solution.py:30
  105.6 2.2 %gather_fusion.1 = f32[32,128]{1,0:T(8,128)S(1)} fusion(f32[4096,128]{1,0:T(8,128)} %bitcast.146, s32[1024]{0:T(1024)S(1)} %pad_clamp_fusion), kind=kCustom, calls=%fused_computation.1 | custom fusion | bytes 32896 | tf_op jit(solution)/shard_map/gather | solution.py:149
  114.3 2.3 %collective-permute-start.8 = (f32[1184,128]{1,0:T(8,128)S(1)}, f32[1184,128]{1,0:T(8,128)}, u32[]{:S(2)}, u32[]{:S(2)}) collective-permute-start(f32[1184,128]{1,0:T(8,128)S(1)} %constant_dynamic-slice_fusion.5), channel_id=1, source_target_pairs={{0,4},{4,0},{8,12},{12,8},{16,20},{20,16},{24,28},{28,24},{32,36},... | collective-permute-start | bytes 1818632 | tf_op jit(solution)/shard_map/ppermute | solution.py:55
  121.0 7.1 %collective-permute-done.9 = f32[592,128]{1,0:T(8,128)S(1)} collective-permute-done((f32[592,128]{1,0:T(8,128)S(1)}, f32[592,128]{1,0:T(8,128)S(1)}, u32[]{:S(2)}, u32[]{:S(2)}) %collective-permute-start.9) | collective-permute-done | bytes 303136 | tf_op jit(solution)/shard_map/ppermute | solution.py:55
  128.2 3.4 %collective-permute-start.10 = (f32[296,128]{1,0:T(8,128)S(1)}, f32[296,128]{1,0:T(8,128)S(1)}, u32[]{:S(2)}, u32[]{:S(2)}) collective-permute-start(f32[296,128]{1,0:T(8,128)S(1)} %constant_dynamic-slice_fusion.3), channel_id=1, source_target_pairs={{0,16},{4,20},{8,24},{12,28},{16,0},{20,4},{24,8},{28,12},{32,48},... | collective-permute-start | bytes 454664 | tf_op jit(solution)/shard_map/ppermute | solution.py:55
  131.6 7.4 %collective-permute-done.10 = f32[296,128]{1,0:T(8,128)S(1)} collective-permute-done((f32[296,128]{1,0:T(8,128)S(1)}, f32[296,128]{1,0:T(8,128)S(1)}, u32[]{:S(2)}, u32[]{:S(2)}) %collective-permute-start.10) | collective-permute-done | bytes 151584 | tf_op jit(solution)/shard_map/ppermute | solution.py:55
  140.7 6.3 %collective-permute-done.11 = f32[148,128]{1,0:T(8,128)S(1)} collective-permute-done((f32[148,128]{1,0:T(8,128)S(1)}, f32[148,128]{1,0:T(8,128)S(1)}, u32[]{:S(2)}, u32[]{:S(2)}) %collective-permute-start.11) | collective-permute-done | bytes 75808 | tf_op jit(solution)/shard_map/ppermute | solution.py:55
  147.1 2.8 %collective-permute-done.12 = f32[74,128]{1,0:T(8,128)S(1)} collective-permute-done((f32[74,128]{1,0:T(8,128)S(1)}, f32[74,128]{1,0:T(8,128)S(1)}, u32[]{:S(2)}, u32[]{:S(2)}) %collective-permute-start.12) | collective-permute-done | bytes 37920 | tf_op jit(solution)/shard_map/ppermute | solution.py:55
  150.8 3.4 %collective-permute-done.13 = f32[37,128]{1,0:T(8,128)S(1)} collective-permute-done((f32[37,128]{1,0:T(8,128)S(1)}, f32[37,128]{1,0:T(8,128)S(1)}, u32[]{:S(2)}, u32[]{:S(2)}) %collective-permute-start.13) | collective-permute-done | bytes 18976 | tf_op jit(solution)/shard_map/ppermute | solution.py:55
  155.1 3.5 %collective-permute-done.14 = f32[69,128]{1,0:T(8,128)S(1)} collective-permute-done((f32[69,128]{1,0:T(8,128)S(1)}, f32[69,128]{1,0:T(8,128)S(1)}, u32[]{:S(2)}, u32[]{:S(2)}) %collective-permute-start.14) | collective-permute-done | bytes 35360 | tf_op jit(solution)/shard_map/ppermute | solution.py:30
  159.6 2.8 %collective-permute-done.15 = f32[138,128]{1,0:T(8,128)S(1)} collective-permute-done((f32[138,128]{1,0:T(8,128)S(1)}, f32[138,128]{1,0:T(8,128)S(1)}, u32[]{:S(2)}, u32[]{:S(2)}) %collective-permute-start.15) | collective-permute-done | bytes 70688 | tf_op jit(solution)/shard_map/ppermute | solution.py:30
  165.8 4.9 %collective-permute-done.16 = f32[276,128]{1,0:T(8,128)S(1)} collective-permute-done((f32[276,128]{1,0:T(8,128)S(1)}, f32[276,128]{1,0:T(8,128)S(1)}, u32[]{:S(2)}, u32[]{:S(2)}) %collective-permute-start.16) | collective-permute-done | bytes 141344 | tf_op jit(solution)/shard_map/ppermute | solution.py:30
  171.6 11.0 %collective-permute-done.17 = f32[552,128]{1,0:T(8,128)S(1)} collective-permute-done((f32[552,128]{1,0:T(8,128)S(1)}, f32[552,128]{1,0:T(8,128)S(1)}, u32[]{:S(2)}, u32[]{:S(2)}) %collective-permute-start.17) | collective-permute-done | bytes 282656 | tf_op jit(solution)/shard_map/ppermute | solution.py:30
  182.9 12.0 %collective-permute-done.18 = f32[1104,128]{1,0:T(8,128)S(1)} collective-permute-done((f32[1104,128]{1,0:T(8,128)S(1)}, f32[1104,128]{1,0:T(8,128)S(1)}, u32[]{:S(2)}, u32[]{:S(2)}) %collective-permute-start.18) | collective-permute-done | bytes 565280 | tf_op jit(solution)/shard_map/ppermute | solution.py:30
  194.9 6.0 %collective-permute-start.19 = (f32[2208,128]{1,0:T(8,128)S(1)}, f32[2208,128]{1,0:T(8,128)S(1)}, u32[]{:S(2)}, u32[]{:S(2)}) collective-permute-start(f32[2208,128]{1,0:T(8,128)S(1)} %constant_dynamic-update-slice_fusion.2), channel_id=1, source_target_pairs={{0,4},{4,0},{8,12},{12,8},{16,20},{20,16},{24,28},{28,24},{32,36},... | collective-permute-start | bytes 3391496 | tf_op jit(solution)/shard_map/ppermute | solution.py:30
  207.9 2.4 %reshape.245 = f32[2368,128]{1,0:T(8,128)} reshape(f32[64,37,128]{2,1,0:T(8,128)} %slice.257) | data formatting | bytes 2424832 | tf_op jit(solution)/shard_map/reshape | solution.py:59
  210.3 2.4 %slice.258 = f32[2304,128]{1,0:T(8,128)} slice(f32[2368,128]{1,0:T(8,128)} %reshape.245), slice={[0:2304], [0:128]} | slice | bytes 2359296 | tf_op jit(solution)/shard_map/slice | solution.py:179
  (203 shorter events, 73.0 us)
Async XLA Ops:
  8.5 14.6 %collective-permute-start.2 = (f32[72,128]{1,0:T(8,128)S(1)}, f32[72,128]{1,0:T(8,128)S(1)}, u32[]{:S(2)}, u32[]{:S(2)}) collective-permute-start(f32[72,128]{1,0:T(8,128)S(1)} %get-tuple-element.67), channel_id=1, source_target_pairs={{0,128},{4,132},{8,136},{12,140},{16,144},{20,148},{24,152},{28,15... | collective-permute-start | bytes 110600 | tf_op jit(solution)/shard_map/ppermute | solution.py:30
  12.1 7.4 %copy-start.1 = (bf16[48,128,256]{2,1,0:T(8,128)(2,1)S(1)}, bf16[48,128,256]{2,1,0:T(8,128)(2,1)}, u32[]{:S(2)}) copy-start(bf16[48,128,256]{2,1,0:T(8,128)(2,1)} %param.15) | copy-start | bytes 9437188
  13.1 6.6 %collective-permute-start = (bf16[14,3,256]{2,1,0:T(4,128)(2,1)S(1)}, bf16[14,3,256]{2,1,0:T(4,128)(2,1)S(1)}, u32[]{:S(2)}, u32[]{:S(2)}) collective-permute-start(bf16[14,3,256]{2,1,0:T(4,128)(2,1)S(1)} %get-tuple-element.47), channel_id=1, source_target_pairs={{0,4},{4,8},{8,12},{12,16},{16,20},{20,24},{24,28},{28,32},{32,36}... | collective-permute-start | bytes 64520 | tf_op jit(solution)/shard_map/ppermute | solution.py:16
  17.5 2.1 copy-start.31
  17.5 5.2 %collective-permute-start.1 = (bf16[14,3,256]{2,1,0:T(4,128)(2,1)S(1)}, bf16[14,3,256]{2,1,0:T(4,128)(2,1)S(1)}, u32[]{:S(2)}, u32[]{:S(2)}) collective-permute-start(bf16[14,3,256]{2,1,0:T(4,128)(2,1)S(1)} %get-tuple-element.48), channel_id=1, source_target_pairs={{4,0},{8,4},{12,8},{16,12},{20,16},{24,20},{28,24},{32,28},{36,32}... | collective-permute-start | bytes 64520 | tf_op jit(solution)/shard_map/ppermute | solution.py:18
  23.2 3.3 %collective-permute-start.3 = (f32[144,128]{1,0:T(8,128)S(1)}, f32[144,128]{1,0:T(8,128)S(1)}, u32[]{:S(2)}, u32[]{:S(2)}) collective-permute-start(f32[144,128]{1,0:T(8,128)S(1)} %constant_dynamic-update-slice_fusion.16), channel_id=1, source_target_pairs={{0,64},{4,68},{8,72},{12,76},{16,80},{20,84},{24,88},{28,92},{32,9... | collective-permute-start | bytes 221192 | tf_op jit(solution)/shard_map/ppermute | solution.py:30
  26.5 35.2 %collective-permute-start.4 = (f32[288,128]{1,0:T(8,128)S(1)}, f32[288,128]{1,0:T(8,128)}, u32[]{:S(2)}, u32[]{:S(2)}) collective-permute-start(f32[288,128]{1,0:T(8,128)S(1)} %constant_dynamic-update-slice_fusion.14), channel_id=1, source_target_pairs={{0,32},{4,36},{8,40},{12,44},{16,48},{20,52},{24,56},{28,60},{32,0... | collective-permute-start | bytes 442376 | tf_op jit(solution)/shard_map/ppermute | solution.py:30
  48.7 1.6 copy-start.28
  62.6 15.5 %copy-start = (s32[64]{0:T(128)S(1)}, s32[64]{0:T(128)}, u32[]{:S(2)}) copy-start(s32[64]{0:T(128)} %constant.336.clone) | copy-start | bytes 772
  62.6 15.1 %collective-permute-start.5 = (f32[576,128]{1,0:T(8,128)S(1)}, f32[576,128]{1,0:T(8,128)S(1)}, u32[]{:S(2)}, u32[]{:S(2)}) collective-permute-start(f32[576,128]{1,0:T(8,128)S(1)} %constant_dynamic-update-slice_fusion.12), channel_id=1, source_target_pairs={{0,16},{4,20},{8,24},{12,28},{16,0},{20,4},{24,8},{28,12},{32,48},... | collective-permute-start | bytes 884744 | tf_op jit(solution)/shard_map/ppermute | solution.py:30
  77.7 13.1 %collective-permute-start.6 = (f32[1152,128]{1,0:T(8,128)S(1)}, f32[1152,128]{1,0:T(8,128)S(1)}, u32[]{:S(2)}, u32[]{:S(2)}) collective-permute-start(f32[1152,128]{1,0:T(8,128)S(1)} %constant_dynamic-update-slice_fusion.10), channel_id=1, source_target_pairs={{0,8},{4,12},{8,0},{12,4},{16,24},{20,28},{24,16},{28,20},{32,40},... | collective-permute-start | bytes 1769480 | tf_op jit(solution)/shard_map/ppermute | solution.py:30
  79.7 16.2 %all-to-all-start = ((bf16[4,6,66,256]{3,2,1,0:T(8,128)(2,1)}), bf16[4,6,66,256]{3,2,1,0:T(8,128)(2,1)S(1)}, u32[]{:S(2)}, u32[]{:S(2)}) async-start(bf16[4,6,66,256]{3,2,1,0:T(8,128)(2,1)} %stack.2), calls=%async_computation | async-start | bytes 1769472 | tf_op jit(solution)/shard_map/all_to_all | solution.py:136
  91.7 10.2 %collective-permute-start.7 = (f32[2304,128]{1,0:T(8,128)}, f32[2304,128]{1,0:T(8,128)}, u32[]{:S(2)}, u32[]{:S(2)}) collective-permute-start(f32[2304,128]{1,0:T(8,128)} %constant_dynamic-update-slice_fusion.8), channel_id=1, source_target_pairs={{0,4},{4,0},{8,12},{12,8},{16,20},{20,16},{24,28},{28,24},{32,36},... | collective-permute-start | bytes 3538952 | tf_op jit(solution)/shard_map/ppermute | solution.py:30
  95.9 1.8 copy-start.29
  97.7 1.8 copy-start.18
  97.7 2.1 copy-start.10
  97.7 2.4 %copy-start.8 = (bf16[24,64,256]{2,1,0:T(8,128)(2,1)}, bf16[24,64,256]{2,1,0:T(8,128)(2,1)S(1)}, u32[]{:S(2)}) copy-start(bf16[24,64,256]{2,1,0:T(8,128)(2,1)S(1)} %get-tuple-element.63) | copy-start | bytes 2359300
  97.7 2.8 %copy-start.6 = (bf16[24,64,256]{2,1,0:T(8,128)(2,1)}, bf16[24,64,256]{2,1,0:T(8,128)(2,1)S(1)}, u32[]{:S(2)}) copy-start(bf16[24,64,256]{2,1,0:T(8,128)(2,1)S(1)} %get-tuple-element.61) | copy-start | bytes 2359300
  97.7 3.2 %copy-start.4 = (bf16[24,64,256]{2,1,0:T(8,128)(2,1)}, bf16[24,64,256]{2,1,0:T(8,128)(2,1)S(1)}, u32[]{:S(2)}) copy-start(bf16[24,64,256]{2,1,0:T(8,128)(2,1)S(1)} %get-tuple-element.62) | copy-start | bytes 2359300
  97.7 3.5 %copy-start.2 = (bf16[24,64,256]{2,1,0:T(8,128)(2,1)}, bf16[24,64,256]{2,1,0:T(8,128)(2,1)S(1)}, u32[]{:S(2)}) copy-start(bf16[24,64,256]{2,1,0:T(8,128)(2,1)S(1)} %get-tuple-element.58) | copy-start | bytes 2359300
  114.3 4.1 %collective-permute-start.8 = (f32[1184,128]{1,0:T(8,128)S(1)}, f32[1184,128]{1,0:T(8,128)}, u32[]{:S(2)}, u32[]{:S(2)}) collective-permute-start(f32[1184,128]{1,0:T(8,128)S(1)} %constant_dynamic-slice_fusion.5), channel_id=1, source_target_pairs={{0,4},{4,0},{8,12},{12,8},{16,20},{20,16},{24,28},{28,24},{32,36},... | collective-permute-start | bytes 1818632 | tf_op jit(solution)/shard_map/ppermute | solution.py:55
  119.6 8.5 %collective-permute-start.9 = (f32[592,128]{1,0:T(8,128)S(1)}, f32[592,128]{1,0:T(8,128)S(1)}, u32[]{:S(2)}, u32[]{:S(2)}) collective-permute-start(f32[592,128]{1,0:T(8,128)S(1)} %constant_dynamic-slice_fusion.4), channel_id=1, source_target_pairs={{0,8},{4,12},{8,0},{12,4},{16,24},{20,28},{24,16},{28,20},{32,40},... | collective-permute-start | bytes 909320 | tf_op jit(solution)/shard_map/ppermute | solution.py:55
  128.2 10.8 %collective-permute-start.10 = (f32[296,128]{1,0:T(8,128)S(1)}, f32[296,128]{1,0:T(8,128)S(1)}, u32[]{:S(2)}, u32[]{:S(2)}) collective-permute-start(f32[296,128]{1,0:T(8,128)S(1)} %constant_dynamic-slice_fusion.3), channel_id=1, source_target_pairs={{0,16},{4,20},{8,24},{12,28},{16,0},{20,4},{24,8},{28,12},{32,48},... | collective-permute-start | bytes 454664 | tf_op jit(solution)/shard_map/ppermute | solution.py:55
  139.0 7.9 %collective-permute-start.11 = (f32[148,128]{1,0:T(8,128)S(1)}, f32[148,128]{1,0:T(8,128)S(1)}, u32[]{:S(2)}, u32[]{:S(2)}) collective-permute-start(f32[148,128]{1,0:T(8,128)S(1)} %constant_dynamic-slice_fusion.2), channel_id=1, source_target_pairs={{0,32},{4,36},{8,40},{12,44},{16,48},{20,52},{24,56},{28,60},{32,0... | collective-permute-start | bytes 227336 | tf_op jit(solution)/shard_map/ppermute | solution.py:55
  147.0 2.9 %collective-permute-start.12 = (f32[74,128]{1,0:T(8,128)S(1)}, f32[74,128]{1,0:T(8,128)S(1)}, u32[]{:S(2)}, u32[]{:S(2)}) collective-permute-start(f32[74,128]{1,0:T(8,128)S(1)} %constant_dynamic-slice_fusion.1), channel_id=1, source_target_pairs={{0,64},{4,68},{8,72},{12,76},{16,80},{20,84},{24,88},{28,92},{32,9... | collective-permute-start | bytes 113672 | tf_op jit(solution)/shard_map/ppermute | solution.py:55
  150.0 4.2 %collective-permute-start.13 = (f32[37,128]{1,0:T(8,128)S(1)}, f32[37,128]{1,0:T(8,128)S(1)}, u32[]{:S(2)}, u32[]{:S(2)}) collective-permute-start(f32[37,128]{1,0:T(8,128)S(1)} %constant_dynamic-slice_fusion), channel_id=1, source_target_pairs={{0,128},{4,132},{8,136},{12,140},{16,144},{20,148},{24,152},{28,15... | collective-permute-start | bytes 56840 | tf_op jit(solution)/shard_map/ppermute | solution.py:55
  154.2 4.4 %collective-permute-start.14 = (f32[69,128]{1,0:T(8,128)S(1)}, f32[69,128]{1,0:T(8,128)S(1)}, u32[]{:S(2)}, u32[]{:S(2)}) collective-permute-start(f32[69,128]{1,0:T(8,128)S(1)} %pad_maximum_fusion.2), channel_id=1, source_target_pairs={{0,128},{4,132},{8,136},{12,140},{16,144},{20,148},{24,152},{28,15... | collective-permute-start | bytes 105992 | tf_op jit(solution)/shard_map/ppermute | solution.py:30
  158.9 3.6 %collective-permute-start.15 = (f32[138,128]{1,0:T(8,128)S(1)}, f32[138,128]{1,0:T(8,128)S(1)}, u32[]{:S(2)}, u32[]{:S(2)}) collective-permute-start(f32[138,128]{1,0:T(8,128)S(1)} %dynamic_update_slice.85), channel_id=1, source_target_pairs={{0,64},{4,68},{8,72},{12,76},{16,80},{20,84},{24,88},{28,92},{32,9... | collective-permute-start | bytes 211976 | tf_op jit(solution)/shard_map/ppermute | solution.py:30
  162.8 7.9 %collective-permute-start.16 = (f32[276,128]{1,0:T(8,128)S(1)}, f32[276,128]{1,0:T(8,128)S(1)}, u32[]{:S(2)}, u32[]{:S(2)}) collective-permute-start(f32[276,128]{1,0:T(8,128)S(1)} %dynamic_update_slice.87), channel_id=1, source_target_pairs={{0,32},{4,36},{8,40},{12,44},{16,48},{20,52},{24,56},{28,60},{32,0... | collective-permute-start | bytes 423944 | tf_op jit(solution)/shard_map/ppermute | solution.py:30
  171.4 11.2 %collective-permute-start.17 = (f32[552,128]{1,0:T(8,128)S(1)}, f32[552,128]{1,0:T(8,128)S(1)}, u32[]{:S(2)}, u32[]{:S(2)}) collective-permute-start(f32[552,128]{1,0:T(8,128)S(1)} %dynamic_update_slice.89), channel_id=1, source_target_pairs={{0,16},{4,20},{8,24},{12,28},{16,0},{20,4},{24,8},{28,12},{32,48},... | collective-permute-start | bytes 847880 | tf_op jit(solution)/shard_map/ppermute | solution.py:30
  182.7 12.2 %collective-permute-start.18 = (f32[1104,128]{1,0:T(8,128)S(1)}, f32[1104,128]{1,0:T(8,128)S(1)}, u32[]{:S(2)}, u32[]{:S(2)}) collective-permute-start(f32[1104,128]{1,0:T(8,128)S(1)} %constant_dynamic-update-slice_fusion.4), channel_id=1, source_target_pairs={{0,8},{4,12},{8,0},{12,4},{16,24},{20,28},{24,16},{28,20},{32,40},... | collective-permute-start | bytes 1695752 | tf_op jit(solution)/shard_map/ppermute | solution.py:30
  194.9 9.0 %collective-permute-start.19 = (f32[2208,128]{1,0:T(8,128)S(1)}, f32[2208,128]{1,0:T(8,128)S(1)}, u32[]{:S(2)}, u32[]{:S(2)}) collective-permute-start(f32[2208,128]{1,0:T(8,128)S(1)} %constant_dynamic-update-slice_fusion.2), channel_id=1, source_target_pairs={{0,4},{4,0},{8,12},{12,8},{16,20},{20,16},{24,28},{28,24},{32,36},... | collective-permute-start | bytes 3391496 | tf_op jit(solution)/shard_map/ppermute | solution.py:30
  (22 other events, 26.3 us)
